TPU v7x, 256 devices: a whole 4x4x8 slice. The times are simulated.
256 devices in a mesh: dp: 8 (over x, core), ctx: 32 (over y, z).
Axes of the slice: x: 4, y: 4, z: 8, core: 2. Of those that a mesh axis runs over, the one named last changes fastest.
Arguments:
- tokens: bfloat16 [32768, 4096], P(('dp', 'ctx')), parts along dimension 0, may hold values from -6 to 6
- pick_flags: int32 [32768], P(('dp', 'ctx')), parts along dimension 0, may hold values from 0 to 1, as said below
- gate_scales: bfloat16 [32768], P(('dp', 'ctx')), parts along dimension 0, may hold values from 0.099609375 to 1
- attn_gain: float32 [4096], replicated, may hold values from 0.4 to 1.6
- query_weight: bfloat16 [4096, 4096], P(None, 'ctx')
- key_weight: bfloat16 [4096, 1024], P(None, 'ctx')
- value_matrix: bfloat16 [4096, 1024], P(None, 'ctx'), may hold values from -0.09375 to 0.09375
- output_weight: bfloat16 [4096, 4096], P('ctx'), may hold values from -0.09375 to 0.09375
- ffn_gain: float32 [4096], replicated, may hold values from 0.25 to 1.75
- gate_weight: bfloat16 [4096, 11264], P(None, 'ctx'), may hold values from -0.09375 to 0.09375
- up_weight: bfloat16 [4096, 11264], P(None, 'ctx'), may hold values from -0.09375 to 0.09375
- down_weight: bfloat16 [11264, 4096], P('ctx'), may hold values from -0.0546875 to 0.0546875
Outputs:
- block_out: bfloat16 [32768, 4096], P(('dp', 'ctx')), parts along dimension 0
There are 8 independent parts, one for each index of `dp`. A program takes and returns all parts, laid end to end along the dimension named above; an argument that names none is the same for every part. Nothing has to cross between parts.
Inputs may be any that keep to these rules, and one draw needn't show every extreme that they name: `pick_flags`: each device's 128 tokens hold at most 32 picks, the first device exactly 32; each document holds exactly 512 picks; a device may hold none.
All inputs are finite; a program needn't handle non-finite values.
Results may differ from a plain program's by a relative error of at most 0.01.
Values may be sent and summed in bfloat16 or wider, within the bound.
A program may use at most 128 MiB of HBM per device.

v0:
```python
import jax
import jax.numpy as jnp
from jax import lax
from jax.sharding import Mesh, PartitionSpec as P

QUERY_HEADS = 32
KEY_VALUE_HEADS = 8
HEAD_SIZE = 128
PICK_DEV = 16
MOST = 32
Z_RUN = 8
GROUP = ("cy", "cz")
norm_eps = 1e-05
rope_base = 500000.0


def rms_scale(matrix, gain_vec):
    mean_square = jnp.mean(matrix * matrix, axis=-1, keepdims=True)
    return matrix * lax.rsqrt(mean_square + norm_eps) * gain_vec


def apply_rotary(values, token_positions):
    half_dim = values.shape[-1] // 2
    frequency = rope_base ** (-(jnp.arange(half_dim, dtype=jnp.float32) * 2.0) / values.shape[-1])
    angles = token_positions.astype(jnp.float32)[:, None] * frequency[None, :]
    cosine = jnp.cos(angles)
    sine_part = jnp.sin(angles)
    lower_half = values[..., :half_dim]
    upper_half = values[..., half_dim:]
    return jnp.concatenate(
        (
            lower_half * cosine - upper_half * sine_part,
            upper_half * cosine + lower_half * sine_part,
        ),
        axis=-1,
    )


def reduce_scatter_rows(partial, y_size, z_size):
    rows, width = partial.shape
    blocks = partial.reshape(z_size, y_size, rows // (y_size * z_size), width)
    over_y = lax.all_to_all(blocks, "cy", 1, 1, tiled=True)
    part = jnp.sum(over_y.astype(jnp.float32), axis=1).astype(jnp.bfloat16)
    over_z = lax.all_to_all(part, "cz", 0, 0, tiled=True)
    return jnp.sum(over_z.astype(jnp.float32), axis=0)


def gather_rows(x):
    return lax.all_gather(lax.all_gather(x, "cy", axis=0, tiled=True), "cz", axis=0, tiled=True)


def body(
    tokens,
    pick_flags,
    gate_scales,
    attn_gain,
    query_weight,
    key_weight,
    value_matrix,
    output_weight,
    ffn_gain,
    gate_weight,
    up_weight,
    down_weight,
):
    tok_local, width = tokens.shape
    y_size = lax.axis_size("cy")
    z_size = lax.axis_size("cz")
    ctx_size = y_size * z_size
    my_index = lax.axis_index("cy") * z_size + lax.axis_index("cz")
    blk = jnp.arange(ctx_size, dtype=jnp.int32)
    block_dev = blk % y_size * z_size + blk // y_size
    picked_count = PICK_DEV * ctx_size
    slots = MOST * ctx_size
    half_pick = PICK_DEV // 2
    half_cycle = ctx_size // 2
    slot_of = jnp.cumsum(pick_flags) - 1
    token_ids = jnp.arange(tok_local, dtype=jnp.int32)
    slot_match = (jnp.arange(MOST, dtype=jnp.int32)[:, None] == slot_of[None, :]) & (
        pick_flags[None, :] == 1
    )
    chosen = jnp.sum(jnp.where(slot_match, token_ids[None, :], 0), axis=1)
    filled = jnp.any(slot_match, axis=1)
    local_index = jnp.where(filled, chosen, -1)
    padded_rows = jnp.where(filled[:, None], tokens[chosen], jnp.zeros((), jnp.bfloat16))
    padded_gate = jnp.where(filled, gate_scales[chosen], jnp.zeros((), jnp.bfloat16))
    lane = jnp.arange(128, dtype=jnp.int32)[None, :]
    extra = jnp.where(
        lane == 0,
        local_index.astype(jnp.bfloat16)[:, None],
        jnp.where(lane == 1, padded_gate[:, None], jnp.zeros((), jnp.bfloat16)),
    )
    packed = jnp.concatenate((padded_rows, extra), axis=1)
    all_packed = gather_rows(packed)
    all_index = all_packed[:, width].astype(jnp.int32)
    slot_filled = all_index >= 0
    counts_blk = jnp.sum(slot_filled.reshape(ctx_size, MOST).astype(jnp.int32), axis=1)
    counts = counts_blk.reshape(z_size, y_size).T.reshape(ctx_size)
    run_ends = jnp.cumsum(counts)
    run_starts = run_ends - counts
    slot_ids = jnp.arange(slots, dtype=jnp.int32)
    slot_pos = block_dev[slot_ids // MOST] * tok_local + all_index
    rope_pos = jnp.where(slot_filled, slot_pos, 0)
    never = jnp.int32(1 << 30)
    mask_pos = jnp.where(slot_filled, slot_pos, never)
    normalized = rms_scale(all_packed[:, :width].astype(jnp.float32), attn_gain).astype(
        jnp.bfloat16
    )
    queries = jnp.dot(normalized, query_weight, preferred_element_type=jnp.float32)
    queries = apply_rotary(queries, rope_pos).astype(jnp.bfloat16)
    kv_weight = jnp.concatenate((key_weight, value_matrix), axis=1)
    kv_local = jnp.einsum(
        "pd,dc->cp", normalized, kv_weight, preferred_element_type=jnp.float32
    ).astype(jnp.bfloat16)
    comps = key_weight.shape[1] // KEY_VALUE_HEADS
    query_group_width = QUERY_HEADS // KEY_VALUE_HEADS
    by_head = jnp.transpose(kv_local.reshape(2, comps, KEY_VALUE_HEADS, slots), (2, 0, 1, 3))
    send = jnp.repeat(by_head, query_group_width, axis=0)
    got = lax.all_to_all(send, GROUP, 0, 0, tiled=True)
    key_cols = got[:, 0].reshape(ctx_size * comps, slots)
    value_cols = got[:, 1].reshape(ctx_size * comps, slots)
    keys_here = apply_rotary(key_cols.T.astype(jnp.float32), rope_pos).astype(jnp.bfloat16)
    values_here = value_cols.T
    scores = jnp.dot(queries, keys_here.T, preferred_element_type=jnp.float32) / jnp.sqrt(
        jnp.float32(HEAD_SIZE)
    )
    allowed = mask_pos[None, :] <= mask_pos[:, None]
    scores = jnp.where(allowed, scores, -jnp.inf)
    row_max = jnp.max(scores, axis=1, keepdims=True)
    exp_terms = jnp.exp(scores - row_max)
    prob_bf = (exp_terms / jnp.sum(exp_terms, axis=1, keepdims=True)).astype(jnp.bfloat16)
    head_pad = jnp.dot(prob_bf, values_here, preferred_element_type=jnp.float32).astype(
        jnp.bfloat16
    )
    order_ids = jnp.arange(picked_count, dtype=jnp.int32)
    owner_of = order_ids // PICK_DEV
    within = order_ids % PICK_DEV
    low_part = within < half_pick
    rank_block = jnp.where(low_part, owner_of, (owner_of + half_cycle) % ctx_size)
    rank_inner = jnp.where(low_part, 2 * within, 2 * (within - half_pick) + 1)
    rank_ids = rank_block * PICK_DEV + rank_inner
    before = (run_ends[None, :] <= rank_ids[:, None]).astype(jnp.int32)
    source = jnp.sum(before, axis=1)
    offset = rank_ids - jnp.sum(before * counts[None, :], axis=1)
    flat_row = (source % z_size * y_size + source // z_size) * MOST + offset
    flat_blocked = flat_row.reshape(ctx_size, PICK_DEV)[block_dev].reshape(picked_count)
    pick_onehot = (flat_blocked[:, None] == slot_ids[None, :]).astype(jnp.bfloat16)
    head_out = jnp.dot(pick_onehot, head_pad, preferred_element_type=jnp.float32).astype(
        jnp.bfloat16
    )
    own_start = my_index * PICK_DEV
    own_flat = lax.dynamic_slice_in_dim(flat_row, own_start, PICK_DEV, 0)
    own_packed = all_packed[own_flat]
    own_rows = own_packed[:, :width].astype(jnp.float32)
    scale_own = own_packed[:, width + 1].astype(jnp.float32)
    attn_own = reduce_scatter_rows(
        jnp.dot(head_out, output_weight, preferred_element_type=jnp.float32).astype(jnp.bfloat16),
        y_size,
        z_size,
    )
    mixed_own = own_rows + attn_own
    normed_own = rms_scale(mixed_own, ffn_gain).astype(jnp.bfloat16)
    normed_ffn = gather_rows(normed_own)
    gate_proj = jnp.dot(normed_ffn, gate_weight, preferred_element_type=jnp.float32)
    up_proj = jnp.dot(normed_ffn, up_weight, preferred_element_type=jnp.float32)
    hidden = (jax.nn.silu(gate_proj) * up_proj).astype(jnp.bfloat16)
    ffn_own = reduce_scatter_rows(
        jnp.dot(hidden, down_weight, preferred_element_type=jnp.float32).astype(jnp.bfloat16),
        y_size,
        z_size,
    )
    final_own = (own_rows + scale_own[:, None] * (attn_own + ffn_own)).astype(jnp.bfloat16)
    own_source = lax.dynamic_slice_in_dim(source, own_start, PICK_DEV, 0)
    targets = jnp.arange(ctx_size, dtype=jnp.int32)[:, None]
    first_half = (own_source[None, :half_pick] == targets)[:, :, None]
    second_half = (own_source[None, half_pick:] == targets)[:, :, None]
    zero = jnp.zeros((), jnp.bfloat16)
    back = jnp.where(
        first_half,
        final_own[None, :half_pick],
        jnp.where(second_half, final_own[None, half_pick:], zero),
    )
    returned = lax.all_to_all(back, GROUP, 0, 0, tiled=True).reshape(ctx_size * half_pick, width)
    my_start = run_starts[my_index]
    rank_here = jnp.clip(my_start + slot_of, 0, picked_count - 1)
    inner_here = rank_here % PICK_DEV
    odd_here = inner_here % 2
    owner_here = (rank_here // PICK_DEV + odd_here * half_cycle) % ctx_size
    take_rows = owner_here * half_pick + inner_here // 2
    return jnp.where(pick_flags[:, None] == 1, returned[take_rows], tokens)


def solution(mesh):
    dp_size, ctx_size = mesh.devices.shape
    z_size = Z_RUN if ctx_size % Z_RUN == 0 else ctx_size
    split = Mesh(mesh.devices.reshape(dp_size, ctx_size // z_size, z_size), ("dp", "cy", "cz"))
    rows = ("dp", "cy", "cz")
    in_specs = (
        P(rows, None),
        P(rows),
        P(rows),
        P(),
        P(None, GROUP),
        P(None, GROUP),
        P(None, GROUP),
        P(GROUP, None),
        P(),
        P(None, GROUP),
        P(None, GROUP),
        P(GROUP, None),
    )
    out_specs = P(rows, None)
    return jax.shard_map(body, mesh=split, in_specs=in_specs, out_specs=out_specs, check_vma=False)
```

profile of v0, /device:TPU:2, one launch (start us, length us, event | category | flops | bytes accessed | tf_op | source)
XLA Modules:
  0.0 529.0 jit_solution(11144931826340381880)
XLA Ops:
  6.5 0.8 broadcast_compare_fusion
  7.4 0.8 copy.32
  8.7 1.4 gather_fusion.1
  10.1 2.3 gather_fusion
  12.6 0.7 pad_maximum_fusion
  13.4 29.7 %all-gather.4.cloned.1.call-done = bf16[128,4224]{1,0:T(8,128)(2,1)} async-done(((bf16[32,4224]{1,0:T(8,128)(2,1)}), bf16[128,4224]{1,0:T(8,128)(2,1)}) %all-gather.4.cloned.1.call-update) | async-done | bytes 1081360 | tf_op jit(solution)/shard_map/all_gather | solution.py:49
  48.6 4.6 select_reduce_fusion
  54.0 15.4 %select_multiply_fusion = s32[1024]{0:T(1024)S(1)} fusion(pred[1024]{0:T(1024)(128)(4,1)S(1)} %fusion.56, pred[1024]{0:T(1024)(128)(4,1)S(1)} %fusion.57, pred[1024]{0:T(1024)(128)(4,1)S(1)} %fusion.80, pred[1024]{0:T(1024)(128)(4,1)S(1)} %fusion.79, pred[1024]{0:T(1024)(128)(4,1)S(1)} %fusion.78, pred[1024]{0:T(1024)(128)(4,1)S(1)} %fusion.77, ...), kind=kLoop, calls=%fused_computation.217 | loop fusion | flops 26624 | bytes 33892 | tf_op jit(solution)/shard_map/mul | solution.py:102
  70.1 72.0 %all-gather.6.cloned.1.call-done = bf16[1024,4224]{1,0:T(8,128)(2,1)} async-done(((bf16[128,4224]{1,0:T(8,128)(2,1)}), bf16[1024,4224]{1,0:T(8,128)(2,1)}) %all-gather.6.cloned.1.call-update) | async-done | bytes 8650768 | tf_op jit(solution)/shard_map/all_gather | solution.py:49
  142.1 1.4 convert_reduce_fusion.2
  144.1 5.1 fusion
  149.3 5.2 fusion.13
  154.5 1.0 broadcast_in_dim.186
  155.6 7.5 %all-to-all-start = ((bf16[32,2,4,1024]{3,2,1,0:T(4,128)(2,1)}), bf16[32,2,4,1024]{3,2,1,0:T(4,128)(2,1)}, u32[]{:S(2)}, u32[]{:S(2)}) async-start(bf16[32,2,4,1024]{3,2,1,0:T(4,128)(2,1)} %bitcast.61), calls=%async_computation | async-start | bytes 1048576 | tf_op jit(solution)/shard_map/all_to_all | solution.py:119
  164.2 1.2 convert_reduce_fusion.4
  165.4 7.2 %fusion.9 = f32[1024,128]{0,1:T(8,128)} fusion(bf16[4096,128]{1,0:T(8,128)(2,1)} %param.16, f32[4096]{0:T(1024)} %param.15, f32[1024]{0:T(1024)S(1)} %add_rsqrt_fusion, bf16[1024,4224]{1,0:T(8,128)(2,1)} %all-gather.6.cloned.1.call-done), kind=kOutput, calls=%fused_computation.25 | convolution fusion | flops 1090519040 | bytes 9981952 | tf_op jit(solution)/shard_map/dot_general | solution.py:109
  172.6 7.1 %all-to-all-done = bf16[32,2,4,1024]{3,2,1,0:T(4,128)(2,1)} async-done(((bf16[32,2,4,1024]{3,2,1,0:T(4,128)(2,1)}), bf16[32,2,4,1024]{3,2,1,0:T(4,128)(2,1)}, u32[]{:S(2)}, u32[]{:S(2)}) %all-to-all-start) | async-done | bytes 524320 | tf_op jit(solution)/shard_map/all_to_all | solution.py:119
  179.7 2.1 slice_convert_fusion
  181.8 1.2 reshape.557
  183.0 1.7 reshape_squeeze.4
  184.7 2.2 fusion.96
  186.9 0.8 fusion.4
  187.8 1.0 fusion.3
  188.8 1.6 fusion.12
  190.4 5.3 convolution_convert_fusion
  195.7 2.5 copy.38
  198.1 49.8 %all_to_all.30 = bf16[8,4,16,4096]{3,2,0,1:T(8,128)(2,1)} all-to-all(bf16[8,4,16,4096]{3,2,0,1:T(8,128)(2,1)S(1)} %copy.38), channel_id=1, replica_groups=mesh['dp'=8,'cy'=4,'cz'=8] {'cy'}, dimensions={1} | all-to-all | bytes 8388608 | tf_op jit(solution)/shard_map/all_to_all | solution.py:42
  247.9 4.2 reduce_sum.120
  252.1 5.7 %all-to-all-start.2 = ((bf16[8,16,4096]{2,1,0:T(8,128)(2,1)}), bf16[8,16,4096]{2,1,0:T(8,128)(2,1)}, u32[]{:S(2)}, u32[]{:S(2)}) async-start(bf16[8,16,4096]{2,1,0:T(8,128)(2,1)} %reduce_sum.120), calls=%async_computation.2 | async-start | bytes 2097152 | tf_op jit(solution)/shard_map/all_to_all | solution.py:44
  258.2 5.3 %gather_fusion.2 = bf16[16,4224]{1,0:T(8,128)(2,1)S(1)} fusion(bf16[1024,4224]{1,0:T(8,128)(2,1)} %all-gather.6.cloned.1.call-done, s32[1024]{0:T(1024)S(1)} %pad_clamp_fusion.2), kind=kCustom, calls=%fused_computation.2 | custom fusion | bytes 270400 | tf_op jit(solution)/shard_map/gather | solution.py:153
  263.5 21.2 %all-to-all-done.2 = bf16[8,16,4096]{2,1,0:T(8,128)(2,1)} async-done(((bf16[8,16,4096]{2,1,0:T(8,128)(2,1)}), bf16[8,16,4096]{2,1,0:T(8,128)(2,1)}, u32[]{:S(2)}, u32[]{:S(2)}) %all-to-all-start.2) | async-done | bytes 1048608 | tf_op jit(solution)/shard_map/all_to_all | solution.py:44
  284.8 1.4 convert_reduce_fusion.1
  286.4 13.5 %all_gather.14 = bf16[64,4096]{1,0:T(8,128)(2,1)} all-gather(bf16[16,4096]{1,0:T(8,128)(2,1)S(1)} %multiply_convert_fusion), channel_id=1, replica_groups=mesh['dp'=8,'cy'=4,'cz'=8] {'cy'}, dimensions={0}, use_global_device_ids=true | all-gather | bytes 655360 | tf_op jit(solution)/shard_map/all_gather | solution.py:49
  300.0 49.8 %all-gather.8.cloned.1.call-done = bf16[512,4096]{1,0:T(8,128)(2,1)} async-done(((bf16[64,4096]{1,0:T(8,128)(2,1)}), bf16[512,4096]{1,0:T(8,128)(2,1)}) %all-gather.8.cloned.1.call-update) | async-done | bytes 4194320 | tf_op jit(solution)/shard_map/all_gather | solution.py:49
  349.8 5.6 %fusion.170 = f32[512,352]{0,1:T(8,128)} fusion(bf16[512,4096]{1,0:T(8,128)(2,1)} %all-gather.8.cloned.1.call-done, bf16[4096,352]{0,1:T(8,128)(2,1)} %param.21), kind=kOutput, calls=%fused_computation.286 | convolution fusion | flops 1476395008 | bytes 7798784 | tf_op jit(solution)/shard_map/dot_general | solution.py:164
  355.4 9.2 %convolution_convert_fusion.1 = bf16[512,4096]{1,0:T(8,128)(2,1)} fusion(bf16[352,4096]{1,0:T(8,128)(2,1)S(1)} %copy-done, bf16[512,4096]{1,0:T(8,128)(2,1)} %all-gather.8.cloned.1.call-done, bf16[4096,352]{0,1:T(8,128)(2,1)} %param.22, f32[512,352]{0,1:T(8,128)} %fusion.170), kind=kOutput, calls=%fused_computation.11 | convolution fusion | flops 2955968512 | bytes 14876672 | tf_op jit(solution)/shard_map/dot_general | solution.py:168
  364.6 2.5 copy.39
  367.1 53.0 %all_to_all.31 = bf16[8,4,16,4096]{3,2,0,1:T(8,128)(2,1)} all-to-all(bf16[8,4,16,4096]{3,2,0,1:T(8,128)(2,1)S(1)} %copy.39), channel_id=1, replica_groups=mesh['dp'=8,'cy'=4,'cz'=8] {'cy'}, dimensions={1} | all-to-all | bytes 8388608 | tf_op jit(solution)/shard_map/all_to_all | solution.py:42
  420.1 4.2 reduce_sum.123
  424.3 4.3 all-to-all-start.4
  429.0 27.4 %all-to-all-done.4 = bf16[8,16,4096]{2,1,0:T(8,128)(2,1)} async-done(((bf16[8,16,4096]{2,1,0:T(8,128)(2,1)}), bf16[8,16,4096]{2,1,0:T(8,128)(2,1)}, u32[]{:S(2)}, u32[]{:S(2)}) %all-to-all-start.4) | async-done | bytes 1048608 | tf_op jit(solution)/shard_map/all_to_all | solution.py:44
  456.3 1.4 convert_reduce_fusion
  457.8 1.7 select_select_fusion
  459.5 5.0 all-to-all-start.5
  465.1 0.9 fusion.113
  466.0 48.7 %all-to-all-done.5 = bf16[32,8,4096]{2,1,0:T(8,128)(2,1)} async-done(((bf16[32,8,4096]{2,1,0:T(8,128)(2,1)}), bf16[32,8,4096]{2,1,0:T(8,128)(2,1)}, u32[]{:S(2)}, u32[]{:S(2)}) %all-to-all-start.5) | async-done | bytes 2097184 | tf_op jit(solution)/shard_map/all_to_all | solution.py:183
  514.8 5.0 gather_fusion.4
  519.8 2.7 broadcast_select_fusion
  (101 shorter events, 11.3 us)
Async XLA Ops:
  6.5 348.9 %copy-start = (bf16[352,4096]{1,0:T(8,128)(2,1)S(1)}, bf16[352,4096]{1,0:T(8,128)(2,1)}, u32[]{:S(2)}) copy-start(bf16[352,4096]{1,0:T(8,128)(2,1)} %param.23) | copy-start | bytes 8650756
  6.5 36.6 %all-gather.4.cloned.1.call-start = ((), (), s32[]{:S(2)}) async-start(), calls=%async_computation.6 | async-start | bytes 1351680 | tf_op jit(solution)/shard_map/all_gather | solution.py:49
  7.4 2.7 copy-start.4
  13.4 128.8 %all-gather.6.cloned.1.call-start = ((), (), s32[]{:S(2)}) async-start(), calls=%async_computation.7 | async-start | bytes 9732096 | tf_op jit(solution)/shard_map/all_gather | solution.py:49
  144.1 5.2 copy-start.6
  144.1 5.2 copy-start.7
  144.1 5.2 copy-start.8
  155.6 24.1 %all-to-all-start = ((bf16[32,2,4,1024]{3,2,1,0:T(4,128)(2,1)}), bf16[32,2,4,1024]{3,2,1,0:T(4,128)(2,1)}, u32[]{:S(2)}, u32[]{:S(2)}) async-start(bf16[32,2,4,1024]{3,2,1,0:T(4,128)(2,1)} %bitcast.61), calls=%async_computation | async-start | bytes 1048576 | tf_op jit(solution)/shard_map/all_to_all | solution.py:119
  165.4 19.3 %copy-start.3 = (f32[64]{0:T(128)S(1)}, f32[64]{0:T(128)}, u32[]{:S(2)}) copy-start(f32[64]{0:T(128)} %multiply_power_fusion) | copy-start | bytes 772
  186.9 1.9 copy-start.1
  247.9 38.4 %copy-start.2 = (f32[4096]{0:T(1024)S(1)}, f32[4096]{0:T(1024)}, u32[]{:S(2)}) copy-start(f32[4096]{0:T(1024)} %param.20) | copy-start | bytes 49156
  252.1 32.6 %all-to-all-start.2 = ((bf16[8,16,4096]{2,1,0:T(8,128)(2,1)}), bf16[8,16,4096]{2,1,0:T(8,128)(2,1)}, u32[]{:S(2)}, u32[]{:S(2)}) async-start(bf16[8,16,4096]{2,1,0:T(8,128)(2,1)} %reduce_sum.120), calls=%async_computation.2 | async-start | bytes 2097152 | tf_op jit(solution)/shard_map/all_to_all | solution.py:44
  257.8 92.0 %all-gather.8.cloned.1.call-start = ((), (), s32[]{:S(2)}) async-start(), calls=%async_computation.8 | async-start | bytes 4718592 | tf_op jit(solution)/shard_map/all_gather | solution.py:49
  424.3 32.0 %all-to-all-start.4 = ((bf16[8,16,4096]{2,1,0:T(8,128)(2,1)}), bf16[8,16,4096]{2,1,0:T(8,128)(2,1)}, u32[]{:S(2)}, u32[]{:S(2)}) async-start(bf16[8,16,4096]{2,1,0:T(8,128)(2,1)} %reduce_sum.123), calls=%async_computation.4 | async-start | bytes 2097152 | tf_op jit(solution)/shard_map/all_to_all | solution.py:44
  459.5 55.3 %all-to-all-start.5 = ((bf16[32,8,4096]{2,1,0:T(8,128)(2,1)}), bf16[32,8,4096]{2,1,0:T(8,128)(2,1)}, u32[]{:S(2)}, u32[]{:S(2)}) async-start(bf16[32,8,4096]{2,1,0:T(8,128)(2,1)} %select_select_fusion), calls=%async_computation.5 | async-start | bytes 4194304 | tf_op jit(solution)/shard_map/all_to_all | solution.py:183
  514.8 5.0 copy-start.5
Sparse Core Ops, SparseCore 0:
  13.5 29.5 all-gather.3
  44.9 97.1 all-gather.5
  300.1 49.6 all-gather.7
where the time goes:
time: 530 us; the launch traced here: 529 us
  waiting for transfers between devices  256 us (48%)
  blocking collectives  116 us (22%)
  other arithmetic  58.1 us (11%)
  matrix products  34.9 us (7%)
  local copies, waits for them, and re-layouts  27.5 us (5%)
  starting transfers between devices  22.8 us (4%)
  between operations  13.4 us (3%)
    all_gather x2, waiting for transfers between devices, gather_rows(): lax.all_gather(lax.all_gather(x, 'cy', axis=0, tiled=True), 'cz', axis=0,...  122 us
    all_to_all x2, blocking collectives, reduce_scatter_rows(): over_y = lax.all_to_all(blocks, 'cy', 1, 1, tiled=True)  103 us
    all_to_all x1, waiting for transfers between devices, body(): lax.all_to_all(back, GROUP, 0, 0, tiled=True)  48.7 us
    all_to_all x2, waiting for transfers between devices, reduce_scatter_rows(): over_z = lax.all_to_all(part, 'cz', 0, 0, tiled=True)  48.6 us
    all_gather x1, waiting for transfers between devices, gather_rows(): lax.all_gather(x, 'cy', axis=0, tiled=True)  29.7 us
    mul x1, other arithmetic, body(): slot_pos = block_dev[slot_ids // MOST] * tok_local + all_index  15.4 us
    all_gather x1, blocking collectives, gather_rows(): lax.all_gather(x, 'cy', axis=0, tiled=True)  13.5 us
  transfers between devices with their start and end apart: 7, of which 7 were waited for; matrix products, arithmetic and copies ran while one was open for 8% of the time, Pallas kernels for 0%

commit v1 on v0

--- a/solution.py
+++ b/solution.py
@@ -46,7 +46,15 @@
 
 
 def gather_rows(x):
-    return lax.all_gather(lax.all_gather(x, "cy", axis=0, tiled=True), "cz", axis=0, tiled=True)
+    return jnp.concatenate(
+        lax.all_to_all(
+            jnp.stack([lax.all_gather(x, "cy", axis=0, tiled=True)] * lax.axis_size("cz")),
+            "cz",
+            0,
+            0,
+        ),
+        axis=0,
+    )
 
 
 def body(

time: 530 us -> 669 us (1.26)
  blocking collectives: 116 us -> 207 us
  waiting for transfers between devices: 256 us -> 293 us
  local copies, waits for them, and re-layouts: 27.5 us -> 34.6 us
    all_to_all x0 -> x1, waiting for transfers between devices: none -> 164 us  [gather_rows(): lax.all_to_all(jnp.stack([lax.all_gather(x, 'cy', axis=0, tiled=True)] *...]
    all_gather x2 -> x0, waiting for transfers between devices: 122 us -> none  [gather_rows(): lax.all_gather(lax.all_gather(x, 'cy', axis=0, tiled=True), 'cz', axis=0,...]
    all_to_all x0 -> x1, blocking collectives: none -> 95.9 us  [gather_rows(): lax.all_to_all(jnp.stack([lax.all_gather(x, 'cy', axis=0, tiled=True)] *...]
    all_to_all x0 -> x1, starting transfers between devices: none -> 7.01 us  [gather_rows(): lax.all_to_all(jnp.stack([lax.all_gather(x, 'cy', axis=0, tiled=True)] *...]
  transfers between devices with their start and end apart: 7 -> 6, of which waited for: 7 -> 6; matrix products, arithmetic and copies ran while one was open for 8% -> 7% of each run, Pallas kernels for 0% -> 0%
where the time goes in v1:
time: 669 us; the launch traced here: 668 us
  waiting for transfers between devices  293 us (44%)
  blocking collectives  207 us (31%)
  other arithmetic  58.3 us (9%)
  local copies, waits for them, and re-layouts  34.6 us (5%)
  matrix products  33 us (5%)
  starting transfers between devices  27.7 us (4%)
  between operations  13.7 us (2%)
    all_to_all x1, waiting for transfers between devices, gather_rows(): lax.all_to_all(jnp.stack([lax.all_gather(x, 'cy', axis=0, tiled=True)] *...  164 us
    all_to_all x2, blocking collectives, reduce_scatter_rows(): over_y = lax.all_to_all(blocks, 'cy', 1, 1, tiled=True)  98 us
    all_to_all x1, blocking collectives, gather_rows(): lax.all_to_all(jnp.stack([lax.all_gather(x, 'cy', axis=0, tiled=True)] *...  95.9 us
    all_to_all x2, waiting for transfers between devices, reduce_scatter_rows(): over_z = lax.all_to_all(part, 'cz', 0, 0, tiled=True)  46.4 us
    all_to_all x1, waiting for transfers between devices, body(): lax.all_to_all(back, GROUP, 0, 0, tiled=True)  45.4 us
    all_gather x1, waiting for transfers between devices, gather_rows(): lax.all_gather(x, 'cy', axis=0, tiled=True)  29.8 us
    mul x1, other arithmetic, body(): slot_pos = block_dev[slot_ids // MOST] * tok_local + all_index  15.6 us
  transfers between devices with their start and end apart: 6, of which 6 were waited for; matrix products, arithmetic and copies ran while one was open for 7% of the time, Pallas kernels for 0%

profile of v1, /device:TPU:2, one launch (start us, length us, event | category | flops | bytes accessed | tf_op | source)
XLA Modules:
  0.0 667.7 jit_solution(14712010532372951164)
XLA Ops:
  7.4 0.8 copy.32
  8.7 1.4 gather_fusion.1
  10.1 2.3 gather_fusion
  13.4 29.8 %all-gather.2.cloned.1.call-done = bf16[128,4224]{1,0:T(8,128)(2,1)} async-done(((bf16[32,4224]{1,0:T(8,128)(2,1)}), bf16[128,4224]{1,0:T(8,128)(2,1)}) %all-gather.2.cloned.1.call-update) | async-done | bytes 1081360 | tf_op jit(solution)/shard_map/all_gather | solution.py:51
  43.1 5.6 stack.4
  48.7 7.0 %all-to-all-start = ((bf16[8,128,4224]{2,1,0:T(8,128)(2,1)}), bf16[8,128,4224]{2,1,0:T(8,128)(2,1)}, u32[]{:S(2)}, u32[]{:S(2)}) async-start(bf16[8,128,4224]{2,1,0:T(8,128)(2,1)} %stack.4), calls=%async_computation | async-start | bytes 17301504 | tf_op jit(solution)/shard_map/all_to_all | solution.py:50
  61.2 4.5 select_reduce_fusion
  66.5 15.6 %select_multiply_fusion = s32[1024]{0:T(1024)S(1)} fusion(pred[1024]{0:T(1024)(128)(4,1)S(1)} %fusion.56, pred[1024]{0:T(1024)(128)(4,1)S(1)} %fusion.57, pred[1024]{0:T(1024)(128)(4,1)S(1)} %fusion.80, pred[1024]{0:T(1024)(128)(4,1)S(1)} %fusion.79, pred[1024]{0:T(1024)(128)(4,1)S(1)} %fusion.78, pred[1024]{0:T(1024)(128)(4,1)S(1)} %fusion.77, ...), kind=kLoop, calls=%fused_computation.217 | loop fusion | flops 26624 | bytes 33892 | tf_op jit(solution)/shard_map/mul | solution.py:110
  83.0 164.1 %all-to-all-done = bf16[8,128,4224]{2,1,0:T(8,128)(2,1)} async-done(((bf16[8,128,4224]{2,1,0:T(8,128)(2,1)}), bf16[8,128,4224]{2,1,0:T(8,128)(2,1)}, u32[]{:S(2)}, u32[]{:S(2)}) %all-to-all-start) | async-done | bytes 8650784 | tf_op jit(solution)/shard_map/all_to_all | solution.py:50
  247.1 1.4 convert_reduce_fusion.2
  249.1 5.1 fusion
  254.3 6.3 fusion.13
  260.8 1.0 broadcast_in_dim.186
  261.8 4.8 all-to-all-start.1
  267.6 1.2 convert_reduce_fusion.4
  268.8 7.2 %fusion.9 = f32[1024,128]{0,1:T(8,128)} fusion(bf16[4096,128]{1,0:T(8,128)(2,1)} %param.16, f32[4096]{0:T(1024)} %param.15, f32[1024]{0:T(1024)S(1)} %add_rsqrt_fusion, bf16[1024,4224]{1,0:T(8,128)(2,1)} %bitcast.3), kind=kOutput, calls=%fused_computation.25 | convolution fusion | flops 1090519040 | bytes 9981952 | tf_op jit(solution)/shard_map/dot_general | solution.py:117
  276.0 7.5 %all-to-all-done.1 = bf16[32,2,4,1024]{3,2,1,0:T(4,128)(2,1)} async-done(((bf16[32,2,4,1024]{3,2,1,0:T(4,128)(2,1)}), bf16[32,2,4,1024]{3,2,1,0:T(4,128)(2,1)}, u32[]{:S(2)}, u32[]{:S(2)}) %all-to-all-start.1) | async-done | bytes 524320 | tf_op jit(solution)/shard_map/all_to_all | solution.py:127
  283.6 2.0 slice_convert_fusion
  286.3 1.2 reshape.569
  287.5 2.2 fusion.96
  289.7 0.8 fusion.4
  290.6 1.0 fusion.3
  291.6 1.6 fusion.12
  293.2 5.3 convolution_convert_fusion
  298.5 2.5 copy.38
  301.0 49.7 %all_to_all.40 = bf16[8,4,16,4096]{3,2,0,1:T(8,128)(2,1)} all-to-all(bf16[8,4,16,4096]{3,2,0,1:T(8,128)(2,1)S(1)} %copy.38), channel_id=1, replica_groups=mesh['dp'=8,'cy'=4,'cz'=8] {'cy'}, dimensions={1} | all-to-all | bytes 8388608 | tf_op jit(solution)/shard_map/all_to_all | solution.py:42
  350.6 4.2 reduce_sum.120
  354.8 6.6 all-to-all-start.3
  361.6 5.3 gather_fusion.2
  366.9 22.2 %all-to-all-done.3 = bf16[8,16,4096]{2,1,0:T(8,128)(2,1)} async-done(((bf16[8,16,4096]{2,1,0:T(8,128)(2,1)}), bf16[8,16,4096]{2,1,0:T(8,128)(2,1)}, u32[]{:S(2)}, u32[]{:S(2)}) %all-to-all-start.3) | async-done | bytes 1048608 | tf_op jit(solution)/shard_map/all_to_all | solution.py:44
  389.1 1.4 convert_reduce_fusion.1
  390.8 13.3 %all_gather.7 = bf16[64,4096]{1,0:T(8,128)(2,1)S(1)} all-gather(bf16[16,4096]{1,0:T(8,128)(2,1)S(1)} %multiply_convert_fusion), channel_id=1, replica_groups=mesh['dp'=8,'cy'=4,'cz'=8] {'cy'}, dimensions={0}, use_global_device_ids=true | all-gather | bytes 655360 | tf_op jit(solution)/shard_map/all_gather | solution.py:51
  404.7 95.9 %all_to_all.41 = bf16[8,64,4096]{2,1,0:T(8,128)(2,1)S(1)} all-to-all(bf16[8,64,4096]{2,1,0:T(8,128)(2,1)S(1)} %stack.5), channel_id=1, replica_groups=mesh['dp'=8,'cy'=4,'cz'=8] {'cz'}, dimensions={0} | all-to-all | bytes 8388608 | tf_op jit(solution)/shard_map/all_to_all | solution.py:50
  500.6 1.9 copy-done.1
  502.5 2.5 fusion.170
  505.1 9.2 %convolution_convert_fusion.1 = bf16[512,4096]{1,0:T(8,128)(2,1)} fusion(bf16[352,4096]{1,0:T(8,128)(2,1)S(1)} %copy-done, bf16[512,4096]{1,0:T(8,128)(2,1)} %bitcast.63, bf16[4096,352]{0,1:T(8,128)(2,1)} %param.22, f32[512,352]{0,1:T(8,128)} %fusion.170), kind=kOutput, calls=%fused_computation.11 | convolution fusion | flops 2955968512 | bytes 14876672 | tf_op jit(solution)/shard_map/dot_general | solution.py:176
  514.2 2.5 copy.39
  516.7 48.3 %all_to_all.42 = bf16[8,4,16,4096]{3,2,0,1:T(8,128)(2,1)} all-to-all(bf16[8,4,16,4096]{3,2,0,1:T(8,128)(2,1)S(1)} %copy.39), channel_id=1, replica_groups=mesh['dp'=8,'cy'=4,'cz'=8] {'cy'}, dimensions={1} | all-to-all | bytes 8388608 | tf_op jit(solution)/shard_map/all_to_all | solution.py:42
  565.0 4.2 reduce_sum.123
  569.3 4.2 all-to-all-start.6
  573.9 24.1 %all-to-all-done.6 = bf16[8,16,4096]{2,1,0:T(8,128)(2,1)} async-done(((bf16[8,16,4096]{2,1,0:T(8,128)(2,1)}), bf16[8,16,4096]{2,1,0:T(8,128)(2,1)}, u32[]{:S(2)}, u32[]{:S(2)}) %all-to-all-start.6) | async-done | bytes 1048608 | tf_op jit(solution)/shard_map/all_to_all | solution.py:44
  598.0 1.4 convert_reduce_fusion
  599.5 1.7 select_select_fusion
  601.2 5.0 all-to-all-start.7
  606.8 0.9 fusion.113
  607.7 45.4 %all-to-all-done.7 = bf16[32,8,4096]{2,1,0:T(8,128)(2,1)} async-done(((bf16[32,8,4096]{2,1,0:T(8,128)(2,1)}), bf16[32,8,4096]{2,1,0:T(8,128)(2,1)}, u32[]{:S(2)}, u32[]{:S(2)}) %all-to-all-start.7) | async-done | bytes 2097184 | tf_op jit(solution)/shard_map/all_to_all | solution.py:191
  653.1 5.0 gather_fusion.4
  658.2 2.7 broadcast_select_fusion
  (98 shorter events, 13.9 us)
Async XLA Ops:
  6.5 498.5 %copy-start = (bf16[352,4096]{1,0:T(8,128)(2,1)S(1)}, bf16[352,4096]{1,0:T(8,128)(2,1)}, u32[]{:S(2)}) copy-start(bf16[352,4096]{1,0:T(8,128)(2,1)} %param.23) | copy-start | bytes 8650756
  6.5 36.6 %all-gather.2.cloned.1.call-start = ((), (), s32[]{:S(2)}) async-start(), calls=%async_computation.8 | async-start | bytes 1351680 | tf_op jit(solution)/shard_map/all_gather | solution.py:51
  7.4 2.7 copy-start.5
  48.7 198.4 %all-to-all-start = ((bf16[8,128,4224]{2,1,0:T(8,128)(2,1)}), bf16[8,128,4224]{2,1,0:T(8,128)(2,1)}, u32[]{:S(2)}, u32[]{:S(2)}) async-start(bf16[8,128,4224]{2,1,0:T(8,128)(2,1)} %stack.4), calls=%async_computation | async-start | bytes 17301504 | tf_op jit(solution)/shard_map/all_to_all | solution.py:50
  261.8 21.7 %all-to-all-start.1 = ((bf16[32,2,4,1024]{3,2,1,0:T(4,128)(2,1)}), bf16[32,2,4,1024]{3,2,1,0:T(4,128)(2,1)}, u32[]{:S(2)}, u32[]{:S(2)}) async-start(bf16[32,2,4,1024]{3,2,1,0:T(4,128)(2,1)} %bitcast.65), calls=%async_computation.1 | async-start | bytes 1048576 | tf_op jit(solution)/shard_map/all_to_all | solution.py:127
  268.8 18.7 %copy-start.4 = (f32[64]{0:T(128)S(1)}, f32[64]{0:T(128)}, u32[]{:S(2)}) copy-start(f32[64]{0:T(128)} %multiply_power_fusion) | copy-start | bytes 772
  289.7 1.9 copy-start.2
  350.6 40.1 %copy-start.3 = (f32[4096]{0:T(1024)S(1)}, f32[4096]{0:T(1024)}, u32[]{:S(2)}) copy-start(f32[4096]{0:T(1024)} %param.20) | copy-start | bytes 49156
  354.8 34.3 %all-to-all-start.3 = ((bf16[8,16,4096]{2,1,0:T(8,128)(2,1)}), bf16[8,16,4096]{2,1,0:T(8,128)(2,1)}, u32[]{:S(2)}, u32[]{:S(2)}) async-start(bf16[8,16,4096]{2,1,0:T(8,128)(2,1)} %reduce_sum.120), calls=%async_computation.3 | async-start | bytes 2097152 | tf_op jit(solution)/shard_map/all_to_all | solution.py:44
  404.6 97.9 %copy-start.7 = (bf16[4096,352]{0,1:T(8,128)(2,1)S(1)}, bf16[4096,352]{0,1:T(8,128)(2,1)}, u32[]{:S(2)}) copy-start(bf16[4096,352]{0,1:T(8,128)(2,1)} %param.21) | copy-start | bytes 8650756
  500.6 1.9 copy-start.1
  569.3 28.7 %all-to-all-start.6 = ((bf16[8,16,4096]{2,1,0:T(8,128)(2,1)}), bf16[8,16,4096]{2,1,0:T(8,128)(2,1)}, u32[]{:S(2)}, u32[]{:S(2)}) async-start(bf16[8,16,4096]{2,1,0:T(8,128)(2,1)} %reduce_sum.123), calls=%async_computation.6 | async-start | bytes 2097152 | tf_op jit(solution)/shard_map/all_to_all | solution.py:44
  601.2 51.9 %all-to-all-start.7 = ((bf16[32,8,4096]{2,1,0:T(8,128)(2,1)}), bf16[32,8,4096]{2,1,0:T(8,128)(2,1)}, u32[]{:S(2)}, u32[]{:S(2)}) async-start(bf16[32,8,4096]{2,1,0:T(8,128)(2,1)} %select_select_fusion), calls=%async_computation.7 | async-start | bytes 4194304 | tf_op jit(solution)/shard_map/all_to_all | solution.py:191
  653.1 5.0 copy-start.6
Sparse Core Ops, SparseCore 0:
  13.5 29.5 all-gather.1
